TPU v7x, 512 devices: a whole 4x4x16 slice. The times are simulated.
512 devices in a mesh: dp: 8 (over z_hi, y), tm: 64 (over z_lo, x, core).
Axes of the slice: x: 4, y: 4, z: 16 (z_hi: 2, z_lo: 8; z = z_hi * 8 + z_lo), core: 2. Of those that a mesh axis runs over, the one named last changes fastest.
Arguments:
- query_proj: bfloat16 [8, 8192, 768], P('dp', 'tm'), may hold values from -240 to 240
- key_proj: bfloat16 [8, 8192, 768], P('dp', 'tm'), may hold values from -6 to 6
- value_proj: bfloat16 [8, 8192, 768], P('dp', 'tm'), may hold values from -6 to 6
- cotangent: bfloat16 [8, 8192, 768], P('dp', 'tm'), may hold values from -6 to 6
- lengths: int32 [8], P('dp'), may hold values from 4096 to 8192, as said below
- rel_bias: float32 [12, 257], replicated, may hold values from -4 to 4
Outputs:
- context: bfloat16 [8, 8192, 768], P('dp', 'tm')
- grad_query: bfloat16 [8, 8192, 768], P('dp', 'tm')
- grad_key: bfloat16 [8, 8192, 768], P('dp', 'tm')
- grad_value: bfloat16 [8, 8192, 768], P('dp', 'tm')
- grad_bias: float32 [12, 257], replicated
Inputs may be any that keep to these rules, and one draw needn't show every extreme that they name: `lengths`: one utterance has all 8192 frames valid and another exactly 4096.
All inputs are finite; a program needn't handle non-finite values.
Results may differ from a plain program's by a relative error of at most 0.005.
Values may be sent and summed in bfloat16 or wider, within the bound.
No kernel may reach another device: no remote copies, remote signals or barrier semaphores. Data moves between devices by JAX's collectives and lax.ppermute only.
A program may use at most 64 MiB of HBM per device.

v0:
```python
import jax
import jax.numpy as jnp
from jax import lax
from jax.sharding import Mesh
from jax.sharding import PartitionSpec as P

H = 12
HD = 64
W = 128
TM = ("tm_0", "tm_1", "tm_2")
DP_TM = ("dp_0", "dp_1", "tm_0", "tm_1", "tm_2")
DP = ("dp_0", "dp_1")
masked_score = -1e30


def padded_2(cells, sides, width):
    for axis, dim in sides:
        count = lax.axis_size(axis)
        ends = count - 1
        head = lax.slice_in_dim(cells, 0, width, axis=dim)
        tail = lax.slice_in_dim(cells, cells.shape[dim] - width, cells.shape[dim], axis=dim)
        cells = jnp.concatenate(
            [
                lax.ppermute(tail, axis, [(i, (i + 1) % count) for i in range(ends)]),
                cells,
                lax.ppermute(head, axis, [((i + 1) % count, i) for i in range(ends)]),
            ],
            axis=dim,
        )
    return cells


def by_axis(x, axes):
    for axis in axes:
        x = lax.psum(x, axis)
    return x


def band_matrix(bias_table, height, breadth):
    num_heads = bias_table.shape[0]
    span_cols = bias_table.shape[1]
    repeated = jnp.broadcast_to(bias_table[:, None, :], (num_heads, height, span_cols))
    padded = jnp.pad(repeated, ((0, 0), (0, 0), (0, breadth + 1 - span_cols)))
    flattened = padded.reshape(num_heads, height * (breadth + 1))[:, : height * breadth]
    return flattened.reshape(num_heads, height, breadth)


def band_sum(values, span_cols):
    num_heads, height, breadth = values.shape
    flattened = jnp.pad(values.reshape(num_heads, height * breadth), ((0, 0), (0, height)))
    return jnp.sum(flattened.reshape(num_heads, height, breadth + 1)[:, :, :span_cols], axis=1)


def heads_first(array, rows):
    return array.reshape(rows, H, HD).transpose(1, 0, 2)


def rows_first(array):
    num_heads, rows, size = array.shape
    return array.transpose(1, 0, 2).reshape(rows, num_heads * size)


def query_side(query_rows, key_rows, value_rows, grad_rows, bias_table, query_pos, key_pos, length):
    scaling = HD ** (-0.5)
    height = query_rows.shape[1]
    breadth = key_rows.shape[1]
    scores = (
        jnp.einsum("hqd,hkd->hqk", query_rows, key_rows, preferred_element_type=jnp.float32)
        * scaling
    )
    scores = scores + band_matrix(bias_table, height, breadth)
    allowed = (
        (jnp.abs(key_pos[None, :] - query_pos[:, None]) <= W)
        & (key_pos[None, :] >= 0)
        & (key_pos[None, :] < length)
    )
    scores = jnp.where(allowed[None], scores, masked_score)
    row_max = jnp.max(scores, axis=-1)
    shifted = jnp.exp(scores - row_max[..., None])
    row_total = jnp.sum(shifted, axis=-1)
    log_total = row_max + jnp.log(row_total)
    attn_probs = shifted / row_total[..., None]
    valid_rows = query_pos < length
    probs_low = attn_probs.astype(jnp.bfloat16)
    mixed = jnp.einsum("hqk,hkd->hqd", probs_low, value_rows, preferred_element_type=jnp.float32)
    context = jnp.where(valid_rows[None, :, None], mixed, 0.0).astype(jnp.bfloat16)
    masked_grad = jnp.where(valid_rows[None, :, None], grad_rows, jnp.zeros_like(grad_rows))
    grad_probs = jnp.einsum(
        "hqd,hkd->hqk", masked_grad, value_rows, preferred_element_type=jnp.float32
    )
    row_delta = jnp.sum(attn_probs * grad_probs, axis=-1)
    grad_scores = attn_probs * (grad_probs - row_delta[..., None])
    grad_low = grad_scores.astype(jnp.bfloat16)
    grad_query = (
        jnp.einsum("hqk,hkd->hqd", grad_low, key_rows, preferred_element_type=jnp.float32) * scaling
    ).astype(jnp.bfloat16)
    grad_table = band_sum(grad_scores, bias_table.shape[1])
    results = (context, grad_query, log_total, row_delta, grad_table)
    return results


def key_side(
    key_rows,
    value_rows,
    query_rows,
    grad_rows,
    log_total,
    row_delta,
    bias_table,
    key_pos,
    query_pos,
    length,
):
    scaling = HD ** (-0.5)
    height = key_rows.shape[1]
    breadth = query_rows.shape[1]
    scores = (
        jnp.einsum("hkd,hqd->hkq", key_rows, query_rows, preferred_element_type=jnp.float32)
        * scaling
    )
    scores = scores + band_matrix(bias_table[:, ::-1], height, breadth)
    valid_query = (query_pos >= 0) & (query_pos < length)
    allowed = (
        (jnp.abs(query_pos[None, :] - key_pos[:, None]) <= W)
        & (key_pos[:, None] < length)
        & valid_query[None, :]
    )
    attn_probs = jnp.where(
        allowed[None], jnp.exp(jnp.where(allowed[None], scores - log_total[:, None, :], 0.0)), 0.0
    )
    probs_low = attn_probs.astype(jnp.bfloat16)
    masked_grad = jnp.where(valid_query[None, :, None], grad_rows, jnp.zeros_like(grad_rows))
    grad_probs = jnp.einsum(
        "hkd,hqd->hkq", value_rows, masked_grad, preferred_element_type=jnp.float32
    )
    grad_scores = attn_probs * (grad_probs - row_delta[:, None, :])
    grad_low = grad_scores.astype(jnp.bfloat16)
    key_grad = (
        jnp.einsum("hkq,hqd->hkd", grad_low, query_rows, preferred_element_type=jnp.float32)
        * scaling
    )
    value_grad = jnp.einsum(
        "hkq,hqd->hkd", probs_low, masked_grad, preferred_element_type=jnp.float32
    )
    return (key_grad, value_grad)


def on_device(query_proj, key_proj, value_proj, cotangent, lengths, rel_bias):
    frames = query_proj.shape[1]
    model_width = query_proj.shape[2]
    extended = frames + 2 * W
    first_frame = lax.axis_index(TM) * frames
    query_pos = first_frame + jnp.arange(frames, dtype=jnp.int32)
    key_pos = first_frame - W + jnp.arange(extended, dtype=jnp.int32)
    length = lengths[0]
    head_group = 4
    groups = H // head_group
    with_rims = padded_2(jnp.stack([key_proj, value_proj, query_proj, cotangent]), ((TM, 2),), W)
    key_ext = heads_first(with_rims[0, 0], extended)
    value_ext = heads_first(with_rims[1, 0], extended)
    query_own = heads_first(query_proj[0], frames)
    grad_own = heads_first(cotangent[0], frames)
    outputs = []
    for group_index in range(groups):
        low_head = group_index * head_group
        high_head = low_head + head_group
        outputs.append(
            query_side(
                query_own[low_head:high_head],
                key_ext[low_head:high_head],
                value_ext[low_head:high_head],
                grad_own[low_head:high_head],
                rel_bias[low_head:high_head],
                query_pos,
                key_pos,
                length,
            )
        )
    context = rows_first(jnp.concatenate([item[0] for item in outputs], axis=0))
    grad_query = rows_first(jnp.concatenate([item[1] for item in outputs], axis=0))
    log_totals = jnp.concatenate([item[2] for item in outputs], axis=0)
    row_deltas = jnp.concatenate([item[3] for item in outputs], axis=0)
    grad_table = jnp.concatenate([item[4] for item in outputs], axis=0)
    row_stats_all = padded_2(jnp.stack([log_totals, row_deltas]), ((TM, 2),), W)
    query_ext = heads_first(with_rims[2, 0], extended)
    grad_ext = heads_first(with_rims[3, 0], extended)
    key_own = heads_first(key_proj[0], frames)
    value_own = heads_first(value_proj[0], frames)
    key_parts = []
    value_parts = []
    for group_index in range(groups):
        low_head = group_index * head_group
        high_head = low_head + head_group
        key_part, value_part = key_side(
            key_own[low_head:high_head],
            value_own[low_head:high_head],
            query_ext[low_head:high_head],
            grad_ext[low_head:high_head],
            row_stats_all[0, low_head:high_head],
            row_stats_all[1, low_head:high_head],
            rel_bias[low_head:high_head],
            query_pos,
            key_pos,
            length,
        )
        key_parts.append(key_part)
        value_parts.append(value_part)
    grad_key = rows_first(jnp.concatenate(key_parts, axis=0)).astype(jnp.bfloat16)
    grad_value = rows_first(jnp.concatenate(value_parts, axis=0)).astype(jnp.bfloat16)
    grad_bias = by_axis(grad_table, DP_TM)
    return (
        context.reshape(1, frames, model_width),
        grad_query.reshape(1, frames, model_width),
        grad_key.reshape(1, frames, model_width),
        grad_value.reshape(1, frames, model_width),
        grad_bias,
    )


def solution(mesh):
    finer = Mesh(mesh.devices.reshape(2, 4, 8, 4, 2), ("dp_0", "dp_1", "tm_0", "tm_1", "tm_2"))
    in_specs = (P(DP, TM, None), P(DP, TM, None), P(DP, TM, None), P(DP, TM, None), P(DP), P())
    out_specs = (P(DP, TM, None), P(DP, TM, None), P(DP, TM, None), P(DP, TM, None), P())
    return jax.shard_map(
        on_device, mesh=finer, in_specs=in_specs, out_specs=out_specs, check_vma=False
    )
```

profile of v0, /device:TPU:1, one launch (start us, length us, event | category | flops | bytes accessed | tf_op | source)
XLA Modules:
  0.0 190.9 jit_solution(16381931620373479713)
XLA Ops:
  0.6 1.1 copy.43
  1.7 1.1 copy.42
  2.8 1.1 copy.41
  3.9 1.2 copy.40
  5.1 1.0 pad_maximum_fusion.1
  6.1 8.7 %collective-permute-start.1 = (bf16[4,1,128,768]{2,3,1,0:T(8,128)(2,1)}, bf16[4,1,128,768]{2,3,1,0:T(8,128)(2,1)}, u32[]{:S(2)}, u32[]{:S(2)}) collective-permute-start(bf16[4,1,128,768]{2,3,1,0:T(8,128)(2,1)} %pad_maximum_fusion.1), channel_id=1, source_target_pairs={{1,0},{2,1},{3,2},{4,3},{5,4},{6,5},{7,6},{8,7},{9,8},{10,9},{11,1... | collective-permute-start | bytes 2359304 | tf_op jit(solution)/shard_map/ppermute | solution.py:26
  14.8 1.9 %collective-permute-start = (bf16[4,1,128,768]{2,3,1,0:T(8,128)(2,1)}, bf16[4,1,128,768]{2,3,1,0:T(8,128)(2,1)}, u32[]{:S(2)}, u32[]{:S(2)}) collective-permute-start(bf16[4,1,128,768]{2,3,1,0:T(8,128)(2,1)} %pad_maximum_fusion.1), channel_id=1, source_target_pairs={{0,1},{1,2},{2,3},{3,4},{4,5},{5,6},{6,7},{7,8},{8,9},{9,10},{10,1... | collective-permute-start | bytes 2359304 | tf_op jit(solution)/shard_map/ppermute | solution.py:24
  17.6 1.0 reshape.263
  19.3 1.0 reshape.261
  20.4 1.1 copy.47
  21.8 1.0 reshape.259
  22.9 1.2 copy.45
  24.6 1.0 reshape.269
  25.8 1.2 copy.67
  27.5 1.0 reshape.267
  28.7 1.2 copy.65
  30.4 1.0 reshape.265
  31.6 1.1 copy.62
  32.7 0.9 and_and_fusion
  33.6 1.6 pad_maximum_fusion
  35.2 1.3 fusion.128
  37.4 0.9 fusion.29
  38.4 0.9 fusion.28
  39.7 1.2 multiply_reduce_fusion.1
  41.4 0.9 fusion.27
  42.3 1.2 multiply_reduce_fusion.2
  44.2 3.3 %collective-permute-start.3 = (f32[2,12,128]{2,1,0:T(8,128)}, f32[2,12,128]{2,1,0:T(8,128)}, u32[]{:S(2)}, u32[]{:S(2)}) collective-permute-start(f32[2,12,128]{2,1,0:T(8,128)} %pad_maximum_fusion.7), channel_id=1, source_target_pairs={{1,0},{2,1},{3,2},{4,3},{5,4},{6,5},{7,6},{8,7},{9,8},{10,9},{11,1... | collective-permute-start | bytes 36872 | tf_op jit(solution)/shard_map/ppermute | solution.py:26
  47.5 2.4 %collective-permute-start.2 = (f32[2,12,128]{2,1,0:T(8,128)}, f32[2,12,128]{2,1,0:T(8,128)}, u32[]{:S(2)}, u32[]{:S(2)}) collective-permute-start(f32[2,12,128]{2,1,0:T(8,128)} %pad_maximum_fusion.7), channel_id=1, source_target_pairs={{0,1},{1,2},{2,3},{3,4},{4,5},{5,6},{6,7},{7,8},{8,9},{9,10},{10,1... | collective-permute-start | bytes 36872 | tf_op jit(solution)/shard_map/ppermute | solution.py:24
  50.3 1.1 copy.74
  51.5 1.3 subtract_multiply_fusion.1
  53.0 1.1 copy.73
  54.1 1.3 subtract_multiply_fusion.2
  56.0 0.8 copy.75
  56.9 0.8 copy.76
  58.4 1.0 reshape.276
  60.2 1.0 reshape.274
  62.0 1.0 reshape.272
  63.1 23.4 %psum.35 = f32[12,257]{1,0:T(8,128)S(1)} all-reduce(f32[12,257]{1,0:T(8,128)S(1)} %pad_maximum_fusion.6), channel_id=1, replica_groups=mesh['dp_0'=2,'dp_1'=4,'tm_0'=8,'tm_1'=4,'tm_2'=2] {'dp_0'}, use_global_device_ids=true, to_apply=%region_12.13 | all-reduce | flops 3084 | bytes 24672 | tf_op jit(solution)/shard_map/psum | solution.py:35
  86.5 13.5 %psum.36 = f32[12,257]{1,0:T(8,128)S(1)} all-reduce(f32[12,257]{1,0:T(8,128)S(1)} %psum.35), channel_id=1, replica_groups=mesh['dp_0'=2,'dp_1'=4,'tm_0'=8,'tm_1'=4,'tm_2'=2] {'dp_1'}, use_global_device_ids=true, to_apply=%region_13.14 | all-reduce | flops 3084 | bytes 24672 | tf_op jit(solution)/shard_map/psum | solution.py:35
  100.0 45.1 %psum.37 = f32[12,257]{1,0:T(8,128)S(1)} all-reduce(f32[12,257]{1,0:T(8,128)S(1)} %psum.36), channel_id=1, replica_groups=mesh['dp_0'=2,'dp_1'=4,'tm_0'=8,'tm_1'=4,'tm_2'=2] {'tm_0'}, use_global_device_ids=true, to_apply=%region_14.15 | all-reduce | flops 3084 | bytes 24672 | tf_op jit(solution)/shard_map/psum | solution.py:35
  145.1 15.4 %psum.38 = f32[12,257]{1,0:T(8,128)S(1)} all-reduce(f32[12,257]{1,0:T(8,128)S(1)} %psum.37), channel_id=1, replica_groups=mesh['dp_0'=2,'dp_1'=4,'tm_0'=8,'tm_1'=4,'tm_2'=2] {'tm_1'}, use_global_device_ids=true, to_apply=%region_15.16 | all-reduce | flops 3084 | bytes 24672 | tf_op jit(solution)/shard_map/psum | solution.py:35
  160.5 19.3 %psum.39 = f32[12,257]{1,0:T(8,128)} all-reduce(f32[12,257]{1,0:T(8,128)S(1)} %psum.38), channel_id=1, replica_groups=mesh['dp_0'=2,'dp_1'=4,'tm_0'=8,'tm_1'=4,'tm_2'=2] {'tm_2'}, use_global_device_ids=true, to_apply=%region_16.17 | all-reduce | flops 3084 | bytes 24672 | tf_op jit(solution)/shard_map/psum | solution.py:35
  179.8 0.8 maximum_bitcast_fusion.5
  180.6 1.6 fusion.5
  184.6 1.7 fusion.35
  186.3 1.7 fusion.34
  189.2 0.8 copy.77
  190.1 0.8 copy.78
  (121 shorter events, 12.3 us)
Async XLA Ops:
  0.6 16.1 %copy-start.20 = (f32[12,257]{1,0:T(8,128)S(1)}, f32[12,257]{1,0:T(8,128)}, u32[]{:S(2)}) copy-start(f32[12,257]{1,0:T(8,128)} %param.11) | copy-start | bytes 37012
  3.9 29.7 %copy-start.5 = (bf16[1,128,768]{1,2,0:T(8,128)(2,1)}, bf16[1,128,768]{1,2,0:T(8,128)(2,1)S(1)}, u32[]{:S(2)}) copy-start(bf16[1,128,768]{1,2,0:T(8,128)(2,1)S(1)} %copy.41) | copy-start | bytes 589828
  5.1 28.5 %copy-start.7 = (bf16[1,128,768]{1,2,0:T(8,128)(2,1)}, bf16[1,128,768]{1,2,0:T(8,128)(2,1)S(1)}, u32[]{:S(2)}) copy-start(bf16[1,128,768]{1,2,0:T(8,128)(2,1)S(1)} %copy.40) | copy-start | bytes 589828
  6.1 27.5 %collective-permute-start.1 = (bf16[4,1,128,768]{2,3,1,0:T(8,128)(2,1)}, bf16[4,1,128,768]{2,3,1,0:T(8,128)(2,1)}, u32[]{:S(2)}, u32[]{:S(2)}) collective-permute-start(bf16[4,1,128,768]{2,3,1,0:T(8,128)(2,1)} %pad_maximum_fusion.1), channel_id=1, source_target_pairs={{1,0},{2,1},{3,2},{4,3},{5,4},{6,5},{7,6},{8,7},{9,8},{10,9},{11,1... | collective-permute-start | bytes 2359304 | tf_op jit(solution)/shard_map/ppermute | solution.py:26
  14.8 18.8 %collective-permute-start = (bf16[4,1,128,768]{2,3,1,0:T(8,128)(2,1)}, bf16[4,1,128,768]{2,3,1,0:T(8,128)(2,1)}, u32[]{:S(2)}, u32[]{:S(2)}) collective-permute-start(bf16[4,1,128,768]{2,3,1,0:T(8,128)(2,1)} %pad_maximum_fusion.1), channel_id=1, source_target_pairs={{0,1},{1,2},{2,3},{3,4},{4,5},{5,6},{6,7},{7,8},{8,9},{9,10},{10,1... | collective-permute-start | bytes 2359304 | tf_op jit(solution)/shard_map/ppermute | solution.py:24
  35.2 1.7 copy-start.1
  39.7 1.2 copy-start
  43.6 6.4 %copy-start.14 = (f32[1,12,128]{2,1,0:T(8,128)}, f32[1,12,128]{2,1,0:T(8,128)S(1)}, u32[]{:S(2)}) copy-start(f32[1,12,128]{2,1,0:T(8,128)S(1)} %maximum_bitcast_fusion) | copy-start | bytes 18436
  44.2 135.6 %collective-permute-start.3 = (f32[2,12,128]{2,1,0:T(8,128)}, f32[2,12,128]{2,1,0:T(8,128)}, u32[]{:S(2)}, u32[]{:S(2)}) collective-permute-start(f32[2,12,128]{2,1,0:T(8,128)} %pad_maximum_fusion.7), channel_id=1, source_target_pairs={{1,0},{2,1},{3,2},{4,3},{5,4},{6,5},{7,6},{8,7},{9,8},{10,9},{11,1... | collective-permute-start | bytes 36872 | tf_op jit(solution)/shard_map/ppermute | solution.py:26
  47.5 132.3 %collective-permute-start.2 = (f32[2,12,128]{2,1,0:T(8,128)}, f32[2,12,128]{2,1,0:T(8,128)}, u32[]{:S(2)}, u32[]{:S(2)}) collective-permute-start(f32[2,12,128]{2,1,0:T(8,128)} %pad_maximum_fusion.7), channel_id=1, source_target_pairs={{0,1},{1,2},{2,3},{3,4},{4,5},{5,6},{6,7},{7,8},{8,9},{9,10},{10,1... | collective-permute-start | bytes 36872 | tf_op jit(solution)/shard_map/ppermute | solution.py:24
  54.1 1.9 copy-start.16
  54.1 1.9 copy-start.17
  54.1 1.9 copy-start.18
  55.5 2.2 %copy-start.2 = (f32[4,128,384]{2,1,0:T(8,128)S(1)}, f32[4,128,384]{2,1,0:T(8,128)}, u32[]{:S(2)}) copy-start(f32[4,128,384]{2,1,0:T(8,128)} %copy.74) | copy-start | bytes 2359300
  58.2 1.3 copy-start.3
  61.8 118.0 %copy-start.15 = (f32[1,12,128]{2,1,0:T(8,128)S(1)}, f32[1,12,128]{2,1,0:T(8,128)}, u32[]{:S(2)}) copy-start(f32[1,12,128]{2,1,0:T(8,128)} %copy-done.14) | copy-start | bytes 18436
  61.8 118.8 %copy-start.8 = (bf16[1,128,768]{1,2,0:T(8,128)(2,1)S(1)}, bf16[1,128,768]{1,2,0:T(8,128)(2,1)}, u32[]{:S(2)}) copy-start(bf16[1,128,768]{1,2,0:T(8,128)(2,1)} %copy-done.7) | copy-start | bytes 589828
  61.8 118.8 %copy-start.13 = (bf16[1,1,384,768]{2,3,1,0:T(8,128)(2,1)S(1)}, bf16[1,1,384,768]{2,3,1,0:T(8,128)(2,1)}, u32[]{:S(2)}) copy-start(bf16[1,1,384,768]{2,3,1,0:T(8,128)(2,1)} %get-tuple-element.18) | copy-start | bytes 1769476
  61.8 118.8 %copy-start.19 = (pred[128,384]{0,1:T(8,128)(4,1)S(1)}, pred[128,384]{0,1:T(8,128)(4,1)}, u32[]{:S(2)}) copy-start(pred[128,384]{0,1:T(8,128)(4,1)} %get-tuple-element.30) | copy-start | bytes 147460
  62.0 120.3 %copy-start.10 = (f32[4,128,384]{1,2,0:T(8,128)S(1)}, f32[4,128,384]{1,2,0:T(8,128)}, u32[]{:S(2)}) copy-start(f32[4,128,384]{1,2,0:T(8,128)} %copy.65) | copy-start | bytes 2359300
  180.6 2.2 %copy-start.4 = (bf16[1,1,384,768]{2,3,1,0:T(8,128)(2,1)S(1)}, bf16[1,1,384,768]{2,3,1,0:T(8,128)(2,1)}, u32[]{:S(2)}) copy-start(bf16[1,1,384,768]{2,3,1,0:T(8,128)(2,1)} %get-tuple-element.17) | copy-start | bytes 1769476
  182.3 1.6 copy-start.12
  182.3 2.3 %copy-start.6 = (bf16[1,128,768]{1,2,0:T(8,128)(2,1)S(1)}, bf16[1,128,768]{1,2,0:T(8,128)(2,1)}, u32[]{:S(2)}) copy-start(bf16[1,128,768]{1,2,0:T(8,128)(2,1)} %copy-done.5) | copy-start | bytes 589828
  182.8 0.9 copy-start.11
  182.8 5.2 %copy-start.9 = (f32[4,128,384]{1,2,0:T(8,128)S(1)}, f32[4,128,384]{1,2,0:T(8,128)}, u32[]{:S(2)}) copy-start(f32[4,128,384]{1,2,0:T(8,128)} %copy.62) | copy-start | bytes 2359300
where the time goes:
time: 192 us; the launch traced here: 191 us
  blocking collectives  117 us (61%)
  local copies, waits for them, and re-layouts  32.3 us (17%)
  starting transfers between devices  16.4 us (9%)
  matrix products  14.2 us (7%)
  other arithmetic  9.12 us (5%)
  between operations  2.11 us (1%)
    psum x5, blocking collectives, by_axis(): x = lax.psum(x, axis)  117 us
    ppermute x2, starting transfers between devices, padded_2(): lax.ppermute(head, axis, [((i + 1) % count, i) for i in range(ends)])  12 us
    unnamed x65, local copies, waits for them, and re-layouts  11.4 us
    reshape x6, local copies, waits for them, and re-layouts, band_matrix(): padded.reshape(num_heads, height * (breadth + 1))[:, :height * breadth]  6.24 us
    reshape x6, local copies, waits for them, and re-layouts, band_matrix(): return flattened.reshape(num_heads, height, breadth)  6.05 us
    ppermute x2, starting transfers between devices, padded_2(): lax.ppermute(tail, axis, [(i, (i + 1) % count) for i in range(ends)])  4.34 us
    dot_general x3, matrix products, key_side(): jnp.einsum('hkq,hqd->hkd', grad_low, query_rows, preferred_element_type=j...  3.87 us
  transfers between devices with their start and end apart: 4, of which 0 were waited for; matrix products, arithmetic and copies ran while one was open for 15% of the time, Pallas kernels for 0%

commit v1 on v0

--- a/solution.py
+++ b/solution.py
@@ -32,7 +32,7 @@
 
 def by_axis(x, axes):
     for axis in axes:
-        x = lax.psum(x, axis)
+        x = jnp.sum(lax.all_gather(x, axis), axis=0)
     return x
 
 

time: 192 us -> 163 us (0.85)
  blocking collectives: 117 us -> 87.1 us
    psum x5 -> x0, blocking collectives: 117 us -> none  [by_axis(): x = lax.psum(x, axis)]
    all_gather x0 -> x5, blocking collectives: none -> 87.1 us  [by_axis(): x = jnp.sum(lax.all_gather(x, axis), axis=0)]
    unnamed x65 -> x67, local copies, waits for them, and re-layouts: 11.4 us -> 10.7 us
  transfers between devices with their start and end apart: 4 -> 4, of which waited for: 0 -> 0; matrix products, arithmetic and copies ran while one was open for 15% -> 19% of each run, Pallas kernels for 0% -> 0%
where the time goes in v1:
time: 163 us
  blocking collectives  87.1 us (53%)
  local copies, waits for them, and re-layouts  32.6 us (20%)
  starting transfers between devices  16.4 us (10%)
  matrix products  14.1 us (9%)
  other arithmetic  10.4 us (6%)
  between operations  2.12 us (1%)
    all_gather x5, blocking collectives, by_axis(): x = jnp.sum(lax.all_gather(x, axis), axis=0)  87.1 us
    ppermute x2, starting transfers between devices, padded_2(): lax.ppermute(head, axis, [((i + 1) % count, i) for i in range(ends)])  12 us
    unnamed x67, local copies, waits for them, and re-layouts  10.7 us
    reshape x6, local copies, waits for them, and re-layouts, band_matrix(): padded.reshape(num_heads, height * (breadth + 1))[:, :height * breadth]  6.24 us
    reshape x6, local copies, waits for them, and re-layouts, band_matrix(): return flattened.reshape(num_heads, height, breadth)  6.05 us
    ppermute x2, starting transfers between devices, padded_2(): lax.ppermute(tail, axis, [(i, (i + 1) % count) for i in range(ends)])  4.34 us
    dot_general x3, matrix products, key_side(): jnp.einsum('hkd,hqd->hkq', key_rows, query_rows, preferred_element_type=j...  3.56 us
    mul x3, local copies, waits for them, and re-layouts, query_side(): grad_scores = attn_probs * (grad_probs - row_delta[..., None])  3.47 us
  transfers between devices with their start and end apart: 4, of which 0 were waited for; matrix products, arithmetic and copies ran while one was open for 19% of the time, Pallas kernels for 0%

profile of v1, /device:TPU:1, one launch (start us, length us, event | category | flops | bytes accessed | tf_op | source)
XLA Modules:
  0.0 162.8 jit_solution(11179882690738038685)
XLA Ops:
  0.6 1.1 copy.82
  1.8 1.2 copy.81
  2.9 1.1 copy.80
  4.0 1.1 copy.79
  5.1 1.0 pad_maximum_fusion.1
  6.1 8.7 %collective-permute-start.1 = (bf16[4,1,128,768]{2,3,1,0:T(8,128)(2,1)}, bf16[4,1,128,768]{2,3,1,0:T(8,128)(2,1)}, u32[]{:S(2)}, u32[]{:S(2)}) collective-permute-start(bf16[4,1,128,768]{2,3,1,0:T(8,128)(2,1)} %pad_maximum_fusion.1), channel_id=1, source_target_pairs={{1,0},{2,1},{3,2},{4,3},{5,4},{6,5},{7,6},{8,7},{9,8},{10,9},{11,1... | collective-permute-start | bytes 2359304 | tf_op jit(solution)/shard_map/ppermute | solution.py:26
  14.8 1.9 %collective-permute-start = (bf16[4,1,128,768]{2,3,1,0:T(8,128)(2,1)}, bf16[4,1,128,768]{2,3,1,0:T(8,128)(2,1)}, u32[]{:S(2)}, u32[]{:S(2)}) collective-permute-start(bf16[4,1,128,768]{2,3,1,0:T(8,128)(2,1)} %pad_maximum_fusion.1), channel_id=1, source_target_pairs={{0,1},{1,2},{2,3},{3,4},{4,5},{5,6},{6,7},{7,8},{8,9},{9,10},{10,1... | collective-permute-start | bytes 2359304 | tf_op jit(solution)/shard_map/ppermute | solution.py:24
  17.6 1.0 reshape.263
  19.3 1.0 reshape.261
  20.4 1.1 copy.86
  21.8 1.0 reshape.259
  22.9 1.2 copy.84
  24.6 1.0 reshape.269
  25.8 1.2 copy.106
  27.5 1.0 reshape.267
  28.7 1.2 copy.104
  30.4 1.0 reshape.265
  31.6 1.1 copy.101
  32.8 0.9 and_and_fusion
  33.7 1.6 pad_maximum_fusion
  35.2 1.3 fusion.128
  37.4 0.9 fusion.29
  38.4 0.9 fusion.28
  39.7 1.2 multiply_reduce_fusion.1
  41.4 0.9 fusion.27
  42.3 1.2 multiply_reduce_fusion.2
  44.2 3.3 %collective-permute-start.3 = (f32[2,12,128]{2,1,0:T(8,128)}, f32[2,12,128]{2,1,0:T(8,128)}, u32[]{:S(2)}, u32[]{:S(2)}) collective-permute-start(f32[2,12,128]{2,1,0:T(8,128)} %pad_maximum_fusion.6), channel_id=1, source_target_pairs={{1,0},{2,1},{3,2},{4,3},{5,4},{6,5},{7,6},{8,7},{9,8},{10,9},{11,1... | collective-permute-start | bytes 36872 | tf_op jit(solution)/shard_map/ppermute | solution.py:26
  47.5 2.4 %collective-permute-start.2 = (f32[2,12,128]{2,1,0:T(8,128)}, f32[2,12,128]{2,1,0:T(8,128)}, u32[]{:S(2)}, u32[]{:S(2)}) collective-permute-start(f32[2,12,128]{2,1,0:T(8,128)} %pad_maximum_fusion.6), channel_id=1, source_target_pairs={{0,1},{1,2},{2,3},{3,4},{4,5},{5,6},{6,7},{7,8},{8,9},{9,10},{10,1... | collective-permute-start | bytes 36872 | tf_op jit(solution)/shard_map/ppermute | solution.py:24
  50.3 1.1 copy.113
  51.5 1.3 subtract_multiply_fusion.1
  53.0 1.2 copy.112
  54.2 1.4 subtract_multiply_fusion.2
  55.8 1.2 copy.111
  57.6 1.0 reshape.276
  59.4 1.0 reshape.274
  61.2 1.0 reshape.272
  62.3 12.1 %all-gather.5 = f32[2,12,257]{2,1,0:T(8,128)S(1)} all-gather(f32[1,12,257]{2,1,0:T(8,128)S(1)} %maximum_bitcast_fusion), channel_id=2, replica_groups=mesh['dp_0'=2,'dp_1'=4,'tm_0'=8,'tm_1'=4,'tm_2'=2] {'dp_0'}, dimensions={0}, use_global_device_ids=true | all-gather | bytes 37008 | tf_op jit(solution)/shard_map/all_gather | solution.py:35
  74.4 9.2 %all-gather.6 = f32[4,12,257]{2,1,0:T(8,128)S(1)} all-gather(f32[1,12,257]{2,1,0:T(8,128)S(1)} %bitcast.241), channel_id=3, replica_groups=mesh['dp_0'=2,'dp_1'=4,'tm_0'=8,'tm_1'=4,'tm_2'=2] {'dp_1'}, dimensions={0}, use_global_device_ids=true | all-gather | bytes 61680 | tf_op jit(solution)/shard_map/all_gather | solution.py:35
  83.6 40.1 %all-gather.7 = f32[8,12,257]{2,1,0:T(8,128)S(1)} all-gather(f32[1,12,257]{2,1,0:T(8,128)S(1)} %bitcast.240), channel_id=4, replica_groups=mesh['dp_0'=2,'dp_1'=4,'tm_0'=8,'tm_1'=4,'tm_2'=2] {'tm_0'}, dimensions={0}, use_global_device_ids=true | all-gather | bytes 111024 | tf_op jit(solution)/shard_map/all_gather | solution.py:35
  123.8 13.5 %all-gather.8 = f32[4,12,257]{2,1,0:T(8,128)S(1)} all-gather(f32[1,12,257]{2,1,0:T(8,128)S(1)} %bitcast.239), channel_id=5, replica_groups=mesh['dp_0'=2,'dp_1'=4,'tm_0'=8,'tm_1'=4,'tm_2'=2] {'tm_1'}, dimensions={0}, use_global_device_ids=true | all-gather | bytes 61680 | tf_op jit(solution)/shard_map/all_gather | solution.py:35
  137.4 0.8 copy.114
  139.0 12.2 %all-gather.9 = f32[2,12,257]{2,1,0:T(8,128)S(1)} all-gather(f32[1,12,257]{2,1,0:T(8,128)S(1)} %bitcast.242), channel_id=6, replica_groups=mesh['dp_0'=2,'dp_1'=4,'tm_0'=8,'tm_1'=4,'tm_2'=2] {'tm_2'}, dimensions={0}, use_global_device_ids=true | all-gather | bytes 37008 | tf_op jit(solution)/shard_map/all_gather | solution.py:35
  151.9 1.4 maximum_bitcast_fusion.6
  153.2 1.4 fusion.5
  154.7 1.7 %fusion.11 = f32[4,128,384]{1,2,0:T(8,128)S(1)} fusion(f32[4,128,384]{1,2,0:T(8,128)S(1)} %copy-done.10, bf16[12,384,64]{1,2,0:T(8,128)(2,1)} %bitcast.228, f32[4,384]{1,0:T(4,128)S(1)} %get-tuple-element.29, pred[128,384]{0,1:T(8,128)(4,1)} %get-tuple-element.35, bf16[12,128,64]{1,2,0:T(8,128)(2,1)S(1)} %bitcast.216), kind=kOutput, calls=%fused_computation.14 | convolution fusion | flops 26148864 | bytes 2283520 | tf_op jit(solution)/shard_map/hkd,hqd->hkq/dot_general | solution.py:118
  157.6 1.7 %fusion.35 = bf16[4,128,64]{1,2,0:T(8,128)(2,1)S(1)} fusion(f32[4,128,384]{1,2,0:T(8,128)} %copy-done.11, f32[4,384]{1,0:T(4,128)S(1)} %get-tuple-element.31, bf16[12,384,64]{1,2,0:T(8,128)(2,1)S(1)} %bitcast.229, bf16[12,384,64]{1,2,0:T(8,128)(2,1)S(1)} %bitcast.204, pred[384]{0:T(512)(128)(4,1)S(1)} %copy-done.19, bf16[12,128,64]{1,2,0:T(8,128)(2,1)S(1)} %bitcast.210), kind=kOutput, calls=%fused_computation.51 | convolution fusion | flops 51085312 | bytes 1317376 | tf_op jit(solution)/shard_map/hkq,hqd->hkd/dot_general | solution.py:139
  161.1 0.8 copy.116
  162.0 0.8 copy.117
  (128 shorter events, 13.0 us)
Async XLA Ops:
  0.6 16.1 %copy-start.17 = (f32[12,257]{1,0:T(8,128)S(1)}, f32[12,257]{1,0:T(8,128)}, u32[]{:S(2)}) copy-start(f32[12,257]{1,0:T(8,128)} %param.11) | copy-start | bytes 37012
  1.7 31.9 %copy-start.6 = (bf16[1,128,768]{1,2,0:T(8,128)(2,1)}, bf16[1,128,768]{1,2,0:T(8,128)(2,1)S(1)}, u32[]{:S(2)}) copy-start(bf16[1,128,768]{1,2,0:T(8,128)(2,1)S(1)} %copy.82) | copy-start | bytes 589828
  6.1 27.5 %collective-permute-start.1 = (bf16[4,1,128,768]{2,3,1,0:T(8,128)(2,1)}, bf16[4,1,128,768]{2,3,1,0:T(8,128)(2,1)}, u32[]{:S(2)}, u32[]{:S(2)}) collective-permute-start(bf16[4,1,128,768]{2,3,1,0:T(8,128)(2,1)} %pad_maximum_fusion.1), channel_id=1, source_target_pairs={{1,0},{2,1},{3,2},{4,3},{5,4},{6,5},{7,6},{8,7},{9,8},{10,9},{11,1... | collective-permute-start | bytes 2359304 | tf_op jit(solution)/shard_map/ppermute | solution.py:26
  14.8 18.8 %collective-permute-start = (bf16[4,1,128,768]{2,3,1,0:T(8,128)(2,1)}, bf16[4,1,128,768]{2,3,1,0:T(8,128)(2,1)}, u32[]{:S(2)}, u32[]{:S(2)}) collective-permute-start(bf16[4,1,128,768]{2,3,1,0:T(8,128)(2,1)} %pad_maximum_fusion.1), channel_id=1, source_target_pairs={{0,1},{1,2},{2,3},{3,4},{4,5},{5,6},{6,7},{7,8},{8,9},{9,10},{10,1... | collective-permute-start | bytes 2359304 | tf_op jit(solution)/shard_map/ppermute | solution.py:24
  32.7 0.9 copy-start.18
  35.2 1.7 %copy-start.1 = (f32[4,128,384]{1,2,0:T(8,128)S(1)}, f32[4,128,384]{1,2,0:T(8,128)}, u32[]{:S(2)}) copy-start(f32[4,128,384]{1,2,0:T(8,128)} %copy.86) | copy-start | bytes 2359300
  38.3 1.1 copy-start.7
  39.7 1.2 copy-start
  44.2 107.6 %collective-permute-start.3 = (f32[2,12,128]{2,1,0:T(8,128)}, f32[2,12,128]{2,1,0:T(8,128)}, u32[]{:S(2)}, u32[]{:S(2)}) collective-permute-start(f32[2,12,128]{2,1,0:T(8,128)} %pad_maximum_fusion.6), channel_id=1, source_target_pairs={{1,0},{2,1},{3,2},{4,3},{5,4},{6,5},{7,6},{8,7},{9,8},{10,9},{11,1... | collective-permute-start | bytes 36872 | tf_op jit(solution)/shard_map/ppermute | solution.py:26
  47.5 104.3 %collective-permute-start.2 = (f32[2,12,128]{2,1,0:T(8,128)}, f32[2,12,128]{2,1,0:T(8,128)}, u32[]{:S(2)}, u32[]{:S(2)}) collective-permute-start(f32[2,12,128]{2,1,0:T(8,128)} %pad_maximum_fusion.6), channel_id=1, source_target_pairs={{0,1},{1,2},{2,3},{3,4},{4,5},{5,6},{6,7},{7,8},{8,9},{9,10},{10,1... | collective-permute-start | bytes 36872 | tf_op jit(solution)/shard_map/ppermute | solution.py:24
  54.2 2.8 %copy-start.2 = (f32[4,128,384]{2,1,0:T(8,128)S(1)}, f32[4,128,384]{2,1,0:T(8,128)}, u32[]{:S(2)}) copy-start(f32[4,128,384]{2,1,0:T(8,128)} %copy.113) | copy-start | bytes 2359300
  57.4 1.3 copy-start.3
  59.2 1.3 copy-start.4
  61.0 62.7 %copy-start.13 = (bf16[4,128,64]{1,2,0:T(8,128)(2,1)S(1)}, bf16[4,128,64]{1,2,0:T(8,128)(2,1)}, u32[]{:S(2)}) copy-start(bf16[4,128,64]{1,2,0:T(8,128)(2,1)} %fusion.29) | copy-start | bytes 196612
  61.0 62.7 %copy-start.14 = (bf16[4,128,64]{1,2,0:T(8,128)(2,1)S(1)}, bf16[4,128,64]{1,2,0:T(8,128)(2,1)}, u32[]{:S(2)}) copy-start(bf16[4,128,64]{1,2,0:T(8,128)(2,1)} %fusion.28) | copy-start | bytes 196612
  61.0 62.7 %copy-start.15 = (bf16[4,128,64]{1,2,0:T(8,128)(2,1)S(1)}, bf16[4,128,64]{1,2,0:T(8,128)(2,1)}, u32[]{:S(2)}) copy-start(bf16[4,128,64]{1,2,0:T(8,128)(2,1)} %fusion.27) | copy-start | bytes 196612
  61.2 92.0 %copy-start.8 = (f32[4,128,384]{1,2,0:T(8,128)S(1)}, f32[4,128,384]{1,2,0:T(8,128)}, u32[]{:S(2)}) copy-start(f32[4,128,384]{1,2,0:T(8,128)} %copy.106) | copy-start | bytes 2359300
  123.7 31.0 %copy-start.10 = (f32[4,128,384]{1,2,0:T(8,128)S(1)}, f32[4,128,384]{1,2,0:T(8,128)}, u32[]{:S(2)}) copy-start(f32[4,128,384]{1,2,0:T(8,128)} %copy.104) | copy-start | bytes 2359300
  153.2 3.2 %copy-start.5 = (bf16[1,1,384,768]{2,3,1,0:T(8,128)(2,1)S(1)}, bf16[1,1,384,768]{2,3,1,0:T(8,128)(2,1)}, u32[]{:S(2)}) copy-start(bf16[1,1,384,768]{2,3,1,0:T(8,128)(2,1)} %get-tuple-element.22) | copy-start | bytes 1769476
  153.2 3.2 %copy-start.19 = (pred[384]{0:T(512)(128)(4,1)S(1)}, pred[384]{0:T(512)(128)(4,1)}, u32[]{:S(2)}) copy-start(pred[384]{0:T(512)(128)(4,1)} %copy-done.18) | copy-start | bytes 1156
  154.7 1.7 %copy-start.11 = (f32[4,128,384]{1,2,0:T(8,128)}, f32[4,128,384]{1,2,0:T(8,128)S(1)}, u32[]{:S(2)}) copy-start(f32[4,128,384]{1,2,0:T(8,128)S(1)} %fusion.5) | copy-start | bytes 2359300
  154.7 2.9 %copy-start.12 = (bf16[1,1,384,768]{2,3,1,0:T(8,128)(2,1)S(1)}, bf16[1,1,384,768]{2,3,1,0:T(8,128)(2,1)}, u32[]{:S(2)}) copy-start(bf16[1,1,384,768]{2,3,1,0:T(8,128)(2,1)} %get-tuple-element.23) | copy-start | bytes 1769476
  156.4 3.4 %copy-start.9 = (f32[4,128,384]{1,2,0:T(8,128)S(1)}, f32[4,128,384]{1,2,0:T(8,128)}, u32[]{:S(2)}) copy-start(f32[4,128,384]{1,2,0:T(8,128)} %copy.101) | copy-start | bytes 2359300
  156.4 3.4 %copy-start.16 = (pred[128,384]{0,1:T(8,128)(4,1)S(1)}, pred[128,384]{0,1:T(8,128)(4,1)}, u32[]{:S(2)}) copy-start(pred[128,384]{0,1:T(8,128)(4,1)} %get-tuple-element.35) | copy-start | bytes 147460
  159.3 1.3 copy-start.20
  159.3 1.3 copy-start.21
